TPU v7x, 32 devices: a whole 2x2x4 slice. The times are simulated.
32 devices in a mesh: grp: 4 (over y, x), dev: 8 (over z, core).
Axes of the slice: x: 2, y: 2, z: 4, core: 2. Of those that a mesh axis runs over, the one named last changes fastest.
Arguments:
- particles: float32 [128, 5, 128], P(('grp', 'dev')), as said below
- entropy: float32 [128, 128], P(('grp', 'dev')), may hold values from 0.5 to 2
- lists: int32 [128, 64], P(('grp', 'dev')), may hold values from 0 to 127, as said below
- counts: int32 [128], P(('grp', 'dev')), may hold values from 16 to 64, as said below
Outputs:
- density: float32 [128, 128], P(('grp', 'dev'))
- accel: float32 [128, 3, 128], P(('grp', 'dev'))
Inputs may be any that keep to these rules, and one draw needn't show every extreme that they name: lists[c, 0] = c; every id lies in the group of c or in one of the two groups next to it, counting groups of 32 cells around a loop. `counts`: each count is a multiple of 16. `particles`: coordinates in 0 to 1 within the group's slab, masses positive, smoothing lengths from 0.3 to 0.6.
All inputs are finite; a program needn't handle non-finite values.
Results may differ from a plain program's by a relative error of at most 0.0003.
Values sent between devices are 32-bit elements; how exact they have to be, the bound alone decides.
No kernel may reach another device: no remote copies, remote signals or barrier semaphores. Data moves between devices by JAX's collectives and lax.ppermute only.
A program may use at most 64 MiB of HBM per device.

v0:
```python
import math
import jax
import jax.numpy as jnp
from jax import lax
from jax.sharding import PartitionSpec as P

NB = 64
NBLK = 8
norm_const = 21.0 / (16.0 * math.pi)


def padded(block, sides, width):
    for axis, dim in sides:
        count = lax.axis_size(axis)
        forward = [(i, i + 1) for i in range(count - 1)]
        forward.append((count - 1, 0))
        backward = [(target, source) for source, target in forward]
        low = lax.ppermute(
            lax.slice_in_dim(block, block.shape[dim] - width, None, axis=dim), axis, forward
        )
        high = lax.ppermute(lax.slice_in_dim(block, 0, width, axis=dim), axis, backward)
        block = jnp.concatenate([low, block, high], axis=dim)
    return block


def kernel_parts(dist_sq, smooth):
    ratio = jnp.sqrt(dist_sq) / smooth
    base_of = jnp.maximum(1.0 - 0.5 * ratio, 0.0)
    kernel = norm_const / smooth**3 * base_of**4 * (1.0 + 2.0 * ratio)
    slope = -5.0 * norm_const / smooth**5 * base_of**3
    return (kernel, slope)


def on_device(particles, entropy, lists, counts):
    own_cells = particles.shape[0]
    groups = lax.axis_size("grp")
    members = lax.axis_size("dev")
    group_cells = own_cells * members
    group_at = lax.axis_index("grp")
    group_of = lists // group_cells
    within = lists % group_cells
    side_of = (group_of - group_at + 1 + groups) % groups
    shift_all = (side_of - 1).astype(jnp.float32)
    member_of = within // own_cells
    cell_of = within % own_cells
    rimmed = padded(particles, (("grp", 0),), own_cells)
    extended = lax.all_gather(rimmed, "dev", axis=0, tiled=True)
    slots_ext = member_of * (3 * own_cells) + side_of * own_cells + cell_of
    upper = NB // NBLK
    slot_range = jnp.arange(NBLK, dtype=jnp.int32)
    own_smooth = particles[:, None, 4, :, None]
    unit_first = jnp.array([1.0, 0.0, 0.0], dtype=jnp.float32)

    def fetch_block(block_at):
        chosen = lax.dynamic_slice_in_dim(slots_ext, block_at * NBLK, NBLK, 1)
        shift_blk = lax.dynamic_slice_in_dim(shift_all, block_at * NBLK, NBLK, 1)
        others = extended[chosen]
        live = ((block_at * NBLK + slot_range)[None, :] < counts[:, None]).astype(jnp.float32)
        offset = particles[:, None, :3, :, None] - others[:, :, :3, None, :]
        offset = offset - shift_blk[:, :, None, None, None] * unit_first[None, None, :, None, None]
        dist_sq = jnp.sum(offset * offset, axis=2)
        return (chosen, others, live, offset, dist_sq)

    def density_step(block_at, total):
        chosen, others, live, offset, dist_sq = fetch_block(block_at)
        kernel, slope = kernel_parts(dist_sq, own_smooth)
        return total + jnp.sum(
            live[:, :, None, None] * others[:, :, 3, None, :] * kernel, axis=(1, 3)
        )

    density = lax.fori_loop(
        0, upper, density_step, jnp.zeros((own_cells, particles.shape[2]), jnp.float32)
    )
    pressure = entropy * density ** (5.0 / 3.0)
    weight = pressure / (density * density)
    weight_rim = padded(weight, (("grp", 0),), own_cells)
    weight_ext = lax.all_gather(weight_rim, "dev", axis=0, tiled=True)

    def force_step(block_at, total):
        chosen, others, live, offset, dist_sq = fetch_block(block_at)
        kernel_i, slope_i = kernel_parts(dist_sq, own_smooth)
        kernel_j, slope_j = kernel_parts(dist_sq, others[:, :, 4, None, :])
        factor = (
            live[:, :, None, None]
            * others[:, :, 3, None, :]
            * (weight[:, None, :, None] * slope_i + weight_ext[chosen][:, :, None, :] * slope_j)
        )
        return total - jnp.sum(factor[:, :, None] * offset, axis=(1, 4))

    accel = lax.fori_loop(
        0, upper, force_step, jnp.zeros((own_cells, 3, particles.shape[2]), jnp.float32)
    )
    return (density, accel)


def solution(mesh):
    return jax.shard_map(
        on_device,
        mesh=mesh,
        in_specs=(
            P(("grp", "dev"), None, None),
            P(("grp", "dev"), None),
            P(("grp", "dev"), None),
            P(("grp", "dev")),
        ),
        out_specs=(P(("grp", "dev"), None), P(("grp", "dev"), None, None)),
        check_vma=False,
    )
```

profile of v0, /device:TPU:0, one launch (start us, length us, event | category | flops | bytes accessed | tf_op | source)
XLA Modules:
  0.0 148.0 jit_solution(8237750292582553730)
XLA Ops:
  1.3 3.9 %collective-permute-start.1 = (f32[4,5,128]{2,1,0:T(8,128)S(1)}, f32[4,5,128]{2,1,0:T(8,128)S(1)}, u32[]{:S(2)}, u32[]{:S(2)}) collective-permute-start(f32[4,5,128]{2,1,0:T(8,128)S(1)} %copy.28), channel_id=1, source_target_pairs={{8,0},{16,8},{24,16},{0,24},{9,1},{17,9},{25,17},{1,25},{10,2},{18... | collective-permute-start | bytes 30728 | tf_op jit(solution)/shard_map/ppermute | solution.py:21
  8.0 1.9 %collective-permute-done = f32[4,5,128]{2,1,0:T(8,128)S(1)} collective-permute-done((f32[4,5,128]{2,1,0:T(8,128)S(1)}, f32[4,5,128]{2,1,0:T(8,128)S(1)}, u32[]{:S(2)}, u32[]{:S(2)}) %collective-permute-start) | collective-permute-done | bytes 10272 | tf_op jit(solution)/shard_map/ppermute | solution.py:18
  9.9 14.7 %all_gather.6 = f32[96,5,128]{2,1,0:T(8,128)S(1)} all-gather(f32[12,5,128]{2,1,0:T(8,128)S(1)} %pad_maximum_fusion), channel_id=1, replica_groups=mesh['grp'=4,'dev'=8] {'dev'}, dimensions={0}, use_global_device_ids=true | all-gather | bytes 276480 | tf_op jit(solution)/shard_map/all_gather | solution.py:47
  24.6 41.9 %while.34 = (s32[]{:T(128)}, f32[4,128]{1,0:T(4,128)S(1)}, s32[4]{0:T(128)}, s32[4,64]{1,0:T(4,128)S(1)}, f32[96,5,128]{2,1,0:T(8,128)S(1)}, /*index=5*/f32[4,1,...) while((s32[]{:T(128)}, f32[4,128]{1,0:T(4,128)S(1)}, ...), condition=%wide.region_3.4_spmd.clone.clone, body=%wide.region_0.3_spmd.sunk.clone.clone.sunk | while | flops 12065039 | bytes 4628909 | solution.py:71
  28.4 1.4 multiply_reduce_fusion.9
  33.7 1.4 multiply_reduce_fusion.9
  38.9 1.4 multiply_reduce_fusion.9
  44.1 1.4 multiply_reduce_fusion.9
  49.4 1.4 multiply_reduce_fusion.9
  54.6 1.4 multiply_reduce_fusion.9
  59.9 1.4 multiply_reduce_fusion.9
  65.1 1.4 multiply_reduce_fusion.9
  68.7 1.6 %collective-permute-done.3 = f32[4,128]{1,0:T(4,128)S(1)} collective-permute-done((f32[4,128]{1,0:T(4,128)S(1)}, f32[4,128]{1,0:T(4,128)S(1)}, u32[]{:S(2)}, u32[]{:S(2)}) %collective-permute-start.3) | collective-permute-done | bytes 2080 | tf_op jit(solution)/shard_map/ppermute | solution.py:21
  70.2 2.0 %collective-permute-done.2 = f32[4,128]{1,0:T(4,128)S(1)} collective-permute-done((f32[4,128]{1,0:T(4,128)S(1)}, f32[4,128]{1,0:T(4,128)S(1)}, u32[]{:S(2)}, u32[]{:S(2)}) %collective-permute-start.2) | collective-permute-done | bytes 2080 | tf_op jit(solution)/shard_map/ppermute | solution.py:18
  72.2 14.0 %all-gather = f32[8,12,128]{2,1,0:T(8,128)S(1)} all-gather(f32[1,12,128]{2,1,0:T(8,128)S(1)} %maximum_bitcast_fusion), channel_id=1, replica_groups=mesh['grp'=4,'dev'=8] {'dev'}, dimensions={0}, use_global_device_ids=true | all-gather | bytes 55296 | tf_op jit(solution)/shard_map/all_gather | solution.py:77
  86.2 61.1 %while.35 = (s32[]{:T(128)}, f32[4,3,128]{2,1,0:T(4,128)S(1)}, s32[4]{0:T(128)}, s32[4,64]{1,0:T(4,128)S(1)}, f32[96,5,128]{2,1,0:T(8,128)S(1)}, /*index=5*/f32[...) while((s32[]{:T(128)}, f32[4,3,128]{2,1,0:T(4,128)S(1)}, ...), condition=%wide.region_7.8_spmd.clone.clone, body=%wide.region_4.7_spmd.sunk.clone.clone.sunk | while | flops 21519628 | bytes 9044925 | solution.py:90
  90.6 1.9 %fusion.24 = f32[4,8,128,128]{3,2,1,0:T(8,128)S(1)} fusion(f32[4,8,128,128]{3,2,1,0:T(8,128)S(1)} %multiply_reduce_fusion.10, f32[4,8,128]{2,1,0:T(8,128)S(1)} %bitcast.59, f32[4,8,128]{2,1,0:T(8,128)S(1)} %get-tuple-element.869, f32[4,8,128]{2,1,0:T(8,128)S(1)} %bitcast.60, f32[4,128]{1,0:T(4,128)S(1)} %bitcast.64, ...), kind=kLoop, calls=%fused_computation.25.clone.1 | loop fusion | flops 9437184 | bytes 4265984 | tf_op jit(solution)/shard_map/while/body/eval_jaxpr/mul | solution.py:84
  92.4 1.4 multiply_reduce_fusion.11
  98.2 1.9 %fusion.24 = f32[4,8,128,128]{3,2,1,0:T(8,128)S(1)} fusion(f32[4,8,128,128]{3,2,1,0:T(8,128)S(1)} %multiply_reduce_fusion.10, f32[4,8,128]{2,1,0:T(8,128)S(1)} %bitcast.59, f32[4,8,128]{2,1,0:T(8,128)S(1)} %get-tuple-element.869, f32[4,8,128]{2,1,0:T(8,128)S(1)} %bitcast.60, f32[4,128]{1,0:T(4,128)S(1)} %bitcast.64, ...), kind=kLoop, calls=%fused_computation.25.clone.1 | loop fusion | flops 9437184 | bytes 4265984 | tf_op jit(solution)/shard_map/while/body/eval_jaxpr/mul | solution.py:84
  100.1 1.4 multiply_reduce_fusion.11
  105.9 1.9 %fusion.24 = f32[4,8,128,128]{3,2,1,0:T(8,128)S(1)} fusion(f32[4,8,128,128]{3,2,1,0:T(8,128)S(1)} %multiply_reduce_fusion.10, f32[4,8,128]{2,1,0:T(8,128)S(1)} %bitcast.59, f32[4,8,128]{2,1,0:T(8,128)S(1)} %get-tuple-element.869, f32[4,8,128]{2,1,0:T(8,128)S(1)} %bitcast.60, f32[4,128]{1,0:T(4,128)S(1)} %bitcast.64, ...), kind=kLoop, calls=%fused_computation.25.clone.1 | loop fusion | flops 9437184 | bytes 4265984 | tf_op jit(solution)/shard_map/while/body/eval_jaxpr/mul | solution.py:84
  107.7 1.4 multiply_reduce_fusion.11
  113.5 1.9 %fusion.24 = f32[4,8,128,128]{3,2,1,0:T(8,128)S(1)} fusion(f32[4,8,128,128]{3,2,1,0:T(8,128)S(1)} %multiply_reduce_fusion.10, f32[4,8,128]{2,1,0:T(8,128)S(1)} %bitcast.59, f32[4,8,128]{2,1,0:T(8,128)S(1)} %get-tuple-element.869, f32[4,8,128]{2,1,0:T(8,128)S(1)} %bitcast.60, f32[4,128]{1,0:T(4,128)S(1)} %bitcast.64, ...), kind=kLoop, calls=%fused_computation.25.clone.1 | loop fusion | flops 9437184 | bytes 4265984 | tf_op jit(solution)/shard_map/while/body/eval_jaxpr/mul | solution.py:84
  115.4 1.4 multiply_reduce_fusion.11
  121.2 1.9 %fusion.24 = f32[4,8,128,128]{3,2,1,0:T(8,128)S(1)} fusion(f32[4,8,128,128]{3,2,1,0:T(8,128)S(1)} %multiply_reduce_fusion.10, f32[4,8,128]{2,1,0:T(8,128)S(1)} %bitcast.59, f32[4,8,128]{2,1,0:T(8,128)S(1)} %get-tuple-element.869, f32[4,8,128]{2,1,0:T(8,128)S(1)} %bitcast.60, f32[4,128]{1,0:T(4,128)S(1)} %bitcast.64, ...), kind=kLoop, calls=%fused_computation.25.clone.1 | loop fusion | flops 9437184 | bytes 4265984 | tf_op jit(solution)/shard_map/while/body/eval_jaxpr/mul | solution.py:84
  123.0 1.4 multiply_reduce_fusion.11
  128.8 1.9 %fusion.24 = f32[4,8,128,128]{3,2,1,0:T(8,128)S(1)} fusion(f32[4,8,128,128]{3,2,1,0:T(8,128)S(1)} %multiply_reduce_fusion.10, f32[4,8,128]{2,1,0:T(8,128)S(1)} %bitcast.59, f32[4,8,128]{2,1,0:T(8,128)S(1)} %get-tuple-element.869, f32[4,8,128]{2,1,0:T(8,128)S(1)} %bitcast.60, f32[4,128]{1,0:T(4,128)S(1)} %bitcast.64, ...), kind=kLoop, calls=%fused_computation.25.clone.1 | loop fusion | flops 9437184 | bytes 4265984 | tf_op jit(solution)/shard_map/while/body/eval_jaxpr/mul | solution.py:84
  130.7 1.4 multiply_reduce_fusion.11
  136.4 1.9 %fusion.24 = f32[4,8,128,128]{3,2,1,0:T(8,128)S(1)} fusion(f32[4,8,128,128]{3,2,1,0:T(8,128)S(1)} %multiply_reduce_fusion.10, f32[4,8,128]{2,1,0:T(8,128)S(1)} %bitcast.59, f32[4,8,128]{2,1,0:T(8,128)S(1)} %get-tuple-element.869, f32[4,8,128]{2,1,0:T(8,128)S(1)} %bitcast.60, f32[4,128]{1,0:T(4,128)S(1)} %bitcast.64, ...), kind=kLoop, calls=%fused_computation.25.clone.1 | loop fusion | flops 9437184 | bytes 4265984 | tf_op jit(solution)/shard_map/while/body/eval_jaxpr/mul | solution.py:84
  138.3 1.4 multiply_reduce_fusion.11
  144.1 1.9 %fusion.24 = f32[4,8,128,128]{3,2,1,0:T(8,128)S(1)} fusion(f32[4,8,128,128]{3,2,1,0:T(8,128)S(1)} %multiply_reduce_fusion.10, f32[4,8,128]{2,1,0:T(8,128)S(1)} %bitcast.59, f32[4,8,128]{2,1,0:T(8,128)S(1)} %get-tuple-element.869, f32[4,8,128]{2,1,0:T(8,128)S(1)} %bitcast.60, f32[4,128]{1,0:T(4,128)S(1)} %bitcast.64, ...), kind=kLoop, calls=%fused_computation.25.clone.1 | loop fusion | flops 9437184 | bytes 4265984 | tf_op jit(solution)/shard_map/while/body/eval_jaxpr/mul | solution.py:84
  145.9 1.4 multiply_reduce_fusion.11
  (268 shorter events, 70.5 us)
Async XLA Ops:
  1.3 6.7 %collective-permute-start.1 = (f32[4,5,128]{2,1,0:T(8,128)S(1)}, f32[4,5,128]{2,1,0:T(8,128)S(1)}, u32[]{:S(2)}, u32[]{:S(2)}) collective-permute-start(f32[4,5,128]{2,1,0:T(8,128)S(1)} %copy.28), channel_id=1, source_target_pairs={{8,0},{16,8},{24,16},{0,24},{9,1},{17,9},{25,17},{1,25},{10,2},{18... | collective-permute-start | bytes 30728 | tf_op jit(solution)/shard_map/ppermute | solution.py:21
  5.3 4.6 %collective-permute-start = (f32[4,5,128]{2,1,0:T(8,128)S(1)}, f32[4,5,128]{2,1,0:T(8,128)S(1)}, u32[]{:S(2)}, u32[]{:S(2)}) collective-permute-start(f32[4,5,128]{2,1,0:T(8,128)S(1)} %copy.28), channel_id=1, source_target_pairs={{0,8},{8,16},{16,24},{24,0},{1,9},{9,17},{17,25},{25,1},{2,10},{10... | collective-permute-start | bytes 30728 | tf_op jit(solution)/shard_map/ppermute | solution.py:18
  24.6 41.9 %copy-start.1 = (f32[4,128]{1,0:T(4,128)S(1)}, f32[4,128]{1,0:T(4,128)}, u32[]{:S(2)}) copy-start(f32[4,128]{1,0:T(4,128)} %param.10) | copy-start | bytes 6148
  66.6 19.7 %copy-start = (f32[4,128]{1,0:T(4,128)}, f32[4,128]{1,0:T(4,128)S(1)}, u32[]{:S(2)}) copy-start(f32[4,128]{1,0:T(4,128)S(1)} %get-tuple-element.691) | copy-start | bytes 6148
  66.6 3.6 %collective-permute-start.3 = (f32[4,128]{1,0:T(4,128)S(1)}, f32[4,128]{1,0:T(4,128)S(1)}, u32[]{:S(2)}, u32[]{:S(2)}) collective-permute-start(f32[4,128]{1,0:T(4,128)S(1)} %multiply_divide_fusion), channel_id=1, source_target_pairs={{8,0},{16,8},{24,16},{0,24},{9,1},{17,9},{25,17},{1,25},{10,2},{18... | collective-permute-start | bytes 6152 | tf_op jit(solution)/shard_map/ppermute | solution.py:21
  67.7 4.5 %collective-permute-start.2 = (f32[4,128]{1,0:T(4,128)S(1)}, f32[4,128]{1,0:T(4,128)S(1)}, u32[]{:S(2)}, u32[]{:S(2)}) collective-permute-start(f32[4,128]{1,0:T(4,128)S(1)} %multiply_divide_fusion), channel_id=1, source_target_pairs={{0,8},{8,16},{16,24},{24,0},{1,9},{9,17},{17,25},{25,1},{2,10},{10... | collective-permute-start | bytes 6152 | tf_op jit(solution)/shard_map/ppermute | solution.py:18
where the time goes:
time: 149 us; the launch traced here: 148 us
  other arithmetic  86.7 us (58%)
  blocking collectives  28.7 us (19%)
  local copies, waits for them, and re-layouts  19.1 us (13%)
  starting transfers between devices  6 us (4%)
  waiting for transfers between devices  5.4 us (4%)
    reduce_sum x16, other arithmetic, fetch_block(): dist_sq = jnp.sum(offset * offset, axis=2)  21.1 us
    mul x8, other arithmetic, force_step(): live[:, :, None, None] * others[:, :, 3, None, :]  14.8 us
    all_gather x1, blocking collectives, on_device(): extended = lax.all_gather(rimmed, 'dev', axis=0, tiled=True)  14.7 us
    all_gather x1, blocking collectives, on_device(): weight_ext = lax.all_gather(weight_rim, 'dev', axis=0, tiled=True)  14 us
    mul x16, other arithmetic, fetch_block(): shift_blk[:, :, None, None, None] * unit_first[None, None, :, None, None]  11.7 us
    convert_element_type x16, other arithmetic, fetch_block(): ((block_at * NBLK + slot_range)[None, :] < counts[:, None]).astype(jnp.fl...  11.7 us
    reduce_sum x8, other arithmetic, density_step(): jnp.sum(live[:, :, None, None] * others[:, :, 3, None, :] * kernel, axis=...  11.5 us
    reduce_sum x8, other arithmetic, force_step(): return total - jnp.sum(factor[:, :, None] * offset, axis=(1, 4))  11.1 us
  transfers between devices with their start and end apart: 4, of which 3 were waited for; matrix products, arithmetic and copies ran while one was open for 2% of the time, Pallas kernels for 0%

commit v1 on v0

--- a/solution.py
+++ b/solution.py
@@ -7,6 +7,23 @@
 NB = 64
 NBLK = 8
 norm_const = 21.0 / (16.0 * math.pi)
+
+
+def laid_out(parts, dim):
+    parts = jnp.moveaxis(parts, 0, dim)
+    shape = parts.shape
+    return parts.reshape(*shape[:dim], shape[dim] * shape[dim + 1], *shape[dim + 2 :])
+
+
+def collected_by_bits(x, axis):
+    peers, index = (lax.axis_size(axis), lax.axis_index(axis))
+    parts, distance = (x[None], 1)
+    while distance < peers:
+        other = lax.ppermute(parts, axis, [(i, i ^ distance) for i in range(peers)])
+        low = index & distance == 0
+        parts = jnp.concatenate([jnp.where(low, parts, other), jnp.where(low, other, parts)])
+        distance *= 2
+    return parts
 
 
 def padded(block, sides, width):
@@ -44,7 +61,7 @@
     member_of = within // own_cells
     cell_of = within % own_cells
     rimmed = padded(particles, (("grp", 0),), own_cells)
-    extended = lax.all_gather(rimmed, "dev", axis=0, tiled=True)
+    extended = laid_out(collected_by_bits(rimmed, "dev"), 0)
     slots_ext = member_of * (3 * own_cells) + side_of * own_cells + cell_of
     upper = NB // NBLK
     slot_range = jnp.arange(NBLK, dtype=jnp.int32)

time: 149 us -> 129 us (0.87)
  other arithmetic: 86.7 us -> 67.2 us
  blocking collectives: 28.7 us -> 14 us
  waiting for transfers between devices: 5.4 us -> 15.1 us
  starting transfers between devices: 6 us -> 10.4 us
    all_gather x1 -> x0, blocking collectives: 14.7 us -> none  [on_device(): extended = lax.all_gather(rimmed, 'dev', axis=0, tiled=True)]
    mul x16, other arithmetic: 11.7 us -> 1.15 us  [fetch_block(): shift_blk[:, :, None, None, None] * unit_first[None, None, :, None, None]]
    convert_element_type x16, other arithmetic: 11.7 us -> 1.15 us  [fetch_block(): ((block_at * NBLK + slot_range)[None, :] < counts[:, None]).astype(jnp.fl...]
    ppermute x0 -> x3, waiting for transfers between devices: none -> 8.56 us  [collected_by_bits(): other = lax.ppermute(parts, axis, [(i, i ^ distance) for i in range(peers)])]
    ppermute x0 -> x3, starting transfers between devices: none -> 4.37 us  [collected_by_bits(): other = lax.ppermute(parts, axis, [(i, i ^ distance) for i in range(peers)])]
  transfers between devices with their start and end apart: 4 -> 7, of which waited for: 3 -> 7; matrix products, arithmetic and copies ran while one was open for 2% -> 3% of each run, Pallas kernels for 0% -> 0%
where the time goes in v1:
time: 129 us; the launch traced here: 128 us
  other arithmetic  67.2 us (52%)
  local copies, waits for them, and re-layouts  19.2 us (15%)
  waiting for transfers between devices  15.1 us (12%)
  blocking collectives  14 us (11%)
  starting transfers between devices  10.4 us (8%)
  loops' own time  1.39 us (1%)
    reduce_sum x16, other arithmetic, fetch_block(): dist_sq = jnp.sum(offset * offset, axis=2)  21.1 us
    mul x8, other arithmetic, force_step(): live[:, :, None, None] * others[:, :, 3, None, :]  14.8 us
    all_gather x1, blocking collectives, on_device(): weight_ext = lax.all_gather(weight_rim, 'dev', axis=0, tiled=True)  14 us
    reduce_sum x8, other arithmetic, density_step(): jnp.sum(live[:, :, None, None] * others[:, :, 3, None, :] * kernel, axis=...  11.5 us
    reduce_sum x8, other arithmetic, force_step(): return total - jnp.sum(factor[:, :, None] * offset, axis=(1, 4))  11.1 us
    gather x16, local copies, waits for them, and re-layouts, fetch_block(): others = extended[chosen]  9.35 us
    ppermute x3, waiting for transfers between devices, collected_by_bits(): other = lax.ppermute(parts, axis, [(i, i ^ distance) for i in range(peers)])  8.56 us
    gather x8, local copies, waits for them, and re-layouts, force_step(): weight_ext[chosen][:, :, None, :] * slope_j  4.59 us
  transfers between devices with their start and end apart: 7, of which 7 were waited for; matrix products, arithmetic and copies ran while one was open for 3% of the time, Pallas kernels for 0%

profile of v1, /device:TPU:0, one launch (start us, length us, event | category | flops | bytes accessed | tf_op | source)
XLA Modules:
  0.0 128.2 jit_solution(3384074377342637397)
XLA Ops:
  0.7 4.0 %collective-permute-start.1 = (f32[4,5,128]{2,0,1:T(4,128)}, f32[4,5,128]{2,0,1:T(4,128)S(1)}, u32[]{:S(2)}, u32[]{:S(2)}) collective-permute-start(f32[4,5,128]{2,0,1:T(4,128)} %param.9), channel_id=1, source_target_pairs={{8,0},{16,8},{24,16},{0,24},{9,1},{17,9},{25,17},{1,25},{10,2},{18... | collective-permute-start | bytes 30728 | tf_op jit(solution)/shard_map/ppermute | solution.py:38
  6.2 3.2 %collective-permute-done = f32[4,5,128]{2,0,1:T(4,128)S(1)} collective-permute-done((f32[4,5,128]{2,0,1:T(4,128)}, f32[4,5,128]{2,0,1:T(4,128)S(1)}, u32[]{:S(2)}, u32[]{:S(2)}) %collective-permute-start) | collective-permute-done | bytes 10272 | tf_op jit(solution)/shard_map/ppermute | solution.py:35
  12.2 1.6 %collective-permute-start.3 = (f32[2,12,5,128]{3,1,2,0:T(8,128)S(1)}, f32[2,12,5,128]{3,1,2,0:T(8,128)S(1)}, u32[]{:S(2)}, u32[]{:S(2)}) collective-permute-start(f32[2,12,5,128]{3,1,2,0:T(8,128)S(1)} %pad_maximum_fusion.2), channel_id=1, source_target_pairs={{0,2},{1,3},{2,0},{3,1},{4,6},{5,7},{6,4},{7,5},{8,10},{9,11},{10,... | collective-permute-start | bytes 184328 | tf_op jit(solution)/shard_map/ppermute | solution.py:22
  15.2 1.5 %collective-permute-done.3 = f32[2,12,5,128]{3,1,2,0:T(8,128)S(1)} collective-permute-done((f32[2,12,5,128]{3,1,2,0:T(8,128)S(1)}, f32[2,12,5,128]{3,1,2,0:T(8,128)S(1)}, u32[]{:S(2)}, u32[]{:S(2)}) %collective-permute-start.3) | collective-permute-done | bytes 61472 | tf_op jit(solution)/shard_map/ppermute | solution.py:22
  16.8 2.7 %collective-permute-start.4 = (f32[4,12,5,128]{3,1,2,0:T(8,128)S(1)}, f32[4,12,5,128]{3,1,2,0:T(8,128)S(1)}, u32[]{:S(2)}, u32[]{:S(2)}) collective-permute-start(f32[4,12,5,128]{3,1,2,0:T(8,128)S(1)} %pad_maximum_fusion.1), channel_id=1, source_target_pairs={{0,4},{1,5},{2,6},{3,7},{4,0},{5,1},{6,2},{7,3},{8,12},{9,13},{10,... | collective-permute-start | bytes 368648 | tf_op jit(solution)/shard_map/ppermute | solution.py:22
  20.1 6.5 %collective-permute-done.4 = f32[4,12,5,128]{3,1,2,0:T(8,128)S(1)} collective-permute-done((f32[4,12,5,128]{3,1,2,0:T(8,128)S(1)}, f32[4,12,5,128]{3,1,2,0:T(8,128)S(1)}, u32[]{:S(2)}, u32[]{:S(2)}) %collective-permute-start.4) | collective-permute-done | bytes 122912 | tf_op jit(solution)/shard_map/ppermute | solution.py:22
  26.9 31.4 %while.34 = (s32[]{:T(128)}, f32[4,128]{1,0:T(4,128)S(1)}, s32[4]{0:T(128)S(1)}, s32[4,64]{1,0:T(4,128)S(1)}, f32[96,5,128]{2,1,0:T(8,128)S(1)}, /*index=5*/f32[...) while((s32[]{:T(128)}, f32[4,128]{1,0:T(4,128)S(1)}, ...), condition=%wide.region_3.4_spmd.clone.clone, body=%wide.region_0.3_spmd.sunk.clone.clone.sunk | while | flops 12065039 | bytes 4628909 | solution.py:88
  29.3 1.4 %multiply_reduce_fusion.9 = f32[4,128]{1,0:T(4,128)S(1)} fusion(f32[4,8,128,128]{3,2,1,0:T(8,128)S(1)} %multiply_reduce_fusion.8, f32[4,128]{1,0:T(4,128)S(1)} %bitcast.71, f32[4,128]{1,0:T(4,128)S(1)} %divide_bitcast_fusion.6, f32[4,8,128]{2,1,0:T(8,128)S(1)} %multiply_bitcast_fusion.3), kind=kLoop, calls=%fused_computation.6.clone.1 | loop fusion | flops 6290944 | bytes 2119680 | tf_op jit(solution)/shard_map/while/body/eval_jaxpr/reduce_sum | solution.py:84
  33.3 1.4 %multiply_reduce_fusion.9 = f32[4,128]{1,0:T(4,128)S(1)} fusion(f32[4,8,128,128]{3,2,1,0:T(8,128)S(1)} %multiply_reduce_fusion.8, f32[4,128]{1,0:T(4,128)S(1)} %bitcast.71, f32[4,128]{1,0:T(4,128)S(1)} %divide_bitcast_fusion.6, f32[4,8,128]{2,1,0:T(8,128)S(1)} %multiply_bitcast_fusion.3), kind=kLoop, calls=%fused_computation.6.clone.1 | loop fusion | flops 6290944 | bytes 2119680 | tf_op jit(solution)/shard_map/while/body/eval_jaxpr/reduce_sum | solution.py:84
  37.2 1.4 %multiply_reduce_fusion.9 = f32[4,128]{1,0:T(4,128)S(1)} fusion(f32[4,8,128,128]{3,2,1,0:T(8,128)S(1)} %multiply_reduce_fusion.8, f32[4,128]{1,0:T(4,128)S(1)} %bitcast.71, f32[4,128]{1,0:T(4,128)S(1)} %divide_bitcast_fusion.6, f32[4,8,128]{2,1,0:T(8,128)S(1)} %multiply_bitcast_fusion.3), kind=kLoop, calls=%fused_computation.6.clone.1 | loop fusion | flops 6290944 | bytes 2119680 | tf_op jit(solution)/shard_map/while/body/eval_jaxpr/reduce_sum | solution.py:84
  41.1 1.4 %multiply_reduce_fusion.9 = f32[4,128]{1,0:T(4,128)S(1)} fusion(f32[4,8,128,128]{3,2,1,0:T(8,128)S(1)} %multiply_reduce_fusion.8, f32[4,128]{1,0:T(4,128)S(1)} %bitcast.71, f32[4,128]{1,0:T(4,128)S(1)} %divide_bitcast_fusion.6, f32[4,8,128]{2,1,0:T(8,128)S(1)} %multiply_bitcast_fusion.3), kind=kLoop, calls=%fused_computation.6.clone.1 | loop fusion | flops 6290944 | bytes 2119680 | tf_op jit(solution)/shard_map/while/body/eval_jaxpr/reduce_sum | solution.py:84
  45.0 1.4 %multiply_reduce_fusion.9 = f32[4,128]{1,0:T(4,128)S(1)} fusion(f32[4,8,128,128]{3,2,1,0:T(8,128)S(1)} %multiply_reduce_fusion.8, f32[4,128]{1,0:T(4,128)S(1)} %bitcast.71, f32[4,128]{1,0:T(4,128)S(1)} %divide_bitcast_fusion.6, f32[4,8,128]{2,1,0:T(8,128)S(1)} %multiply_bitcast_fusion.3), kind=kLoop, calls=%fused_computation.6.clone.1 | loop fusion | flops 6290944 | bytes 2119680 | tf_op jit(solution)/shard_map/while/body/eval_jaxpr/reduce_sum | solution.py:84
  49.0 1.4 %multiply_reduce_fusion.9 = f32[4,128]{1,0:T(4,128)S(1)} fusion(f32[4,8,128,128]{3,2,1,0:T(8,128)S(1)} %multiply_reduce_fusion.8, f32[4,128]{1,0:T(4,128)S(1)} %bitcast.71, f32[4,128]{1,0:T(4,128)S(1)} %divide_bitcast_fusion.6, f32[4,8,128]{2,1,0:T(8,128)S(1)} %multiply_bitcast_fusion.3), kind=kLoop, calls=%fused_computation.6.clone.1 | loop fusion | flops 6290944 | bytes 2119680 | tf_op jit(solution)/shard_map/while/body/eval_jaxpr/reduce_sum | solution.py:84
  52.9 1.4 %multiply_reduce_fusion.9 = f32[4,128]{1,0:T(4,128)S(1)} fusion(f32[4,8,128,128]{3,2,1,0:T(8,128)S(1)} %multiply_reduce_fusion.8, f32[4,128]{1,0:T(4,128)S(1)} %bitcast.71, f32[4,128]{1,0:T(4,128)S(1)} %divide_bitcast_fusion.6, f32[4,8,128]{2,1,0:T(8,128)S(1)} %multiply_bitcast_fusion.3), kind=kLoop, calls=%fused_computation.6.clone.1 | loop fusion | flops 6290944 | bytes 2119680 | tf_op jit(solution)/shard_map/while/body/eval_jaxpr/reduce_sum | solution.py:84
  56.8 1.4 %multiply_reduce_fusion.9 = f32[4,128]{1,0:T(4,128)S(1)} fusion(f32[4,8,128,128]{3,2,1,0:T(8,128)S(1)} %multiply_reduce_fusion.8, f32[4,128]{1,0:T(4,128)S(1)} %bitcast.71, f32[4,128]{1,0:T(4,128)S(1)} %divide_bitcast_fusion.6, f32[4,8,128]{2,1,0:T(8,128)S(1)} %multiply_bitcast_fusion.3), kind=kLoop, calls=%fused_computation.6.clone.1 | loop fusion | flops 6290944 | bytes 2119680 | tf_op jit(solution)/shard_map/while/body/eval_jaxpr/reduce_sum | solution.py:84
  58.4 2.0 %collective-permute-start.5 = (f32[4,128]{1,0:T(4,128)S(1)}, f32[4,128]{1,0:T(4,128)S(1)}, u32[]{:S(2)}, u32[]{:S(2)}) collective-permute-start(f32[4,128]{1,0:T(4,128)S(1)} %multiply_divide_fusion), channel_id=1, source_target_pairs={{0,8},{8,16},{16,24},{24,0},{1,9},{9,17},{17,25},{25,1},{2,10},{10... | collective-permute-start | bytes 6152 | tf_op jit(solution)/shard_map/ppermute | solution.py:35
  60.4 1.6 %collective-permute-done.6 = f32[4,128]{1,0:T(4,128)S(1)} collective-permute-done((f32[4,128]{1,0:T(4,128)S(1)}, f32[4,128]{1,0:T(4,128)S(1)}, u32[]{:S(2)}, u32[]{:S(2)}) %collective-permute-start.6) | collective-permute-done | bytes 2080 | tf_op jit(solution)/shard_map/ppermute | solution.py:38
  62.9 14.0 %all-gather = f32[8,12,128]{2,1,0:T(8,128)S(1)} all-gather(f32[1,12,128]{2,1,0:T(8,128)S(1)} %maximum_bitcast_fusion.1), channel_id=1, replica_groups=mesh['grp'=4,'dev'=8] {'dev'}, dimensions={0}, use_global_device_ids=true | all-gather | bytes 55296 | tf_op jit(solution)/shard_map/all_gather | solution.py:94
  76.9 50.6 %while.35 = (s32[]{:T(128)}, f32[4,3,128]{2,1,0:T(4,128)S(1)}, s32[4]{0:T(128)S(1)}, s32[4,64]{1,0:T(4,128)S(1)}, f32[96,5,128]{2,1,0:T(8,128)S(1)}, /*index=5*/...) while((s32[]{:T(128)}, f32[4,3,128]{2,1,0:T(4,128)S(1)}, ...), condition=%wide.region_7.8_spmd.clone.clone, body=%wide.region_4.7_spmd.sunk.clone.clone.sunk | while | flops 21519628 | bytes 9044925 | solution.py:107
  80.0 1.9 %fusion.24 = f32[4,8,128,128]{3,2,1,0:T(8,128)S(1)} fusion(f32[4,8,128,128]{3,2,1,0:T(8,128)S(1)} %multiply_reduce_fusion.10, f32[4,8,128]{2,1,0:T(8,128)S(1)} %bitcast.67, f32[4,8,128]{2,1,0:T(8,128)S(1)} %get-tuple-element.875, f32[4,8,128]{2,1,0:T(8,128)S(1)} %bitcast.68, f32[4,128]{1,0:T(4,128)S(1)} %bitcast.72, ...), kind=kLoop, calls=%fused_computation.25.clone.1 | loop fusion | flops 9437184 | bytes 4265984 | tf_op jit(solution)/shard_map/while/body/eval_jaxpr/mul | solution.py:101
  81.8 1.4 %multiply_reduce_fusion.11 = f32[4,3,128]{2,1,0:T(4,128)S(1)} fusion(f32[4,8,128,128]{3,2,1,0:T(8,128)S(1)} %fusion.24, f32[4,8,3]{2,1,0:T(8,128)S(1)} %broadcast_multiply_fusion.5, f32[4,8,3,128]{3,2,1,0:T(4,128)S(1)} %slice.124, f32[4,3,128]{2,1,0:T(4,128)S(1)} %slice.125), kind=kLoop, calls=%fused_computation.17.clone.1 | loop fusion | flops 6289920 | bytes 2158976 | tf_op jit(solution)/shard_map/while/body/eval_jaxpr/reduce_sum | solution.py:105
  86.3 1.9 %fusion.24 = f32[4,8,128,128]{3,2,1,0:T(8,128)S(1)} fusion(f32[4,8,128,128]{3,2,1,0:T(8,128)S(1)} %multiply_reduce_fusion.10, f32[4,8,128]{2,1,0:T(8,128)S(1)} %bitcast.67, f32[4,8,128]{2,1,0:T(8,128)S(1)} %get-tuple-element.875, f32[4,8,128]{2,1,0:T(8,128)S(1)} %bitcast.68, f32[4,128]{1,0:T(4,128)S(1)} %bitcast.72, ...), kind=kLoop, calls=%fused_computation.25.clone.1 | loop fusion | flops 9437184 | bytes 4265984 | tf_op jit(solution)/shard_map/while/body/eval_jaxpr/mul | solution.py:101
  88.2 1.4 %multiply_reduce_fusion.11 = f32[4,3,128]{2,1,0:T(4,128)S(1)} fusion(f32[4,8,128,128]{3,2,1,0:T(8,128)S(1)} %fusion.24, f32[4,8,3]{2,1,0:T(8,128)S(1)} %broadcast_multiply_fusion.5, f32[4,8,3,128]{3,2,1,0:T(4,128)S(1)} %slice.124, f32[4,3,128]{2,1,0:T(4,128)S(1)} %slice.125), kind=kLoop, calls=%fused_computation.17.clone.1 | loop fusion | flops 6289920 | bytes 2158976 | tf_op jit(solution)/shard_map/while/body/eval_jaxpr/reduce_sum | solution.py:105
  92.6 1.9 %fusion.24 = f32[4,8,128,128]{3,2,1,0:T(8,128)S(1)} fusion(f32[4,8,128,128]{3,2,1,0:T(8,128)S(1)} %multiply_reduce_fusion.10, f32[4,8,128]{2,1,0:T(8,128)S(1)} %bitcast.67, f32[4,8,128]{2,1,0:T(8,128)S(1)} %get-tuple-element.875, f32[4,8,128]{2,1,0:T(8,128)S(1)} %bitcast.68, f32[4,128]{1,0:T(4,128)S(1)} %bitcast.72, ...), kind=kLoop, calls=%fused_computation.25.clone.1 | loop fusion | flops 9437184 | bytes 4265984 | tf_op jit(solution)/shard_map/while/body/eval_jaxpr/mul | solution.py:101
  99.0 1.9 %fusion.24 = f32[4,8,128,128]{3,2,1,0:T(8,128)S(1)} fusion(f32[4,8,128,128]{3,2,1,0:T(8,128)S(1)} %multiply_reduce_fusion.10, f32[4,8,128]{2,1,0:T(8,128)S(1)} %bitcast.67, f32[4,8,128]{2,1,0:T(8,128)S(1)} %get-tuple-element.875, f32[4,8,128]{2,1,0:T(8,128)S(1)} %bitcast.68, f32[4,128]{1,0:T(4,128)S(1)} %bitcast.72, ...), kind=kLoop, calls=%fused_computation.25.clone.1 | loop fusion | flops 9437184 | bytes 4265984 | tf_op jit(solution)/shard_map/while/body/eval_jaxpr/mul | solution.py:101
  100.8 1.4 %multiply_reduce_fusion.11 = f32[4,3,128]{2,1,0:T(4,128)S(1)} fusion(f32[4,8,128,128]{3,2,1,0:T(8,128)S(1)} %fusion.24, f32[4,8,3]{2,1,0:T(8,128)S(1)} %broadcast_multiply_fusion.5, f32[4,8,3,128]{3,2,1,0:T(4,128)S(1)} %slice.124, f32[4,3,128]{2,1,0:T(4,128)S(1)} %slice.125), kind=kLoop, calls=%fused_computation.17.clone.1 | loop fusion | flops 6289920 | bytes 2158976 | tf_op jit(solution)/shard_map/while/body/eval_jaxpr/reduce_sum | solution.py:105
  105.3 1.9 %fusion.24 = f32[4,8,128,128]{3,2,1,0:T(8,128)S(1)} fusion(f32[4,8,128,128]{3,2,1,0:T(8,128)S(1)} %multiply_reduce_fusion.10, f32[4,8,128]{2,1,0:T(8,128)S(1)} %bitcast.67, f32[4,8,128]{2,1,0:T(8,128)S(1)} %get-tuple-element.875, f32[4,8,128]{2,1,0:T(8,128)S(1)} %bitcast.68, f32[4,128]{1,0:T(4,128)S(1)} %bitcast.72, ...), kind=kLoop, calls=%fused_computation.25.clone.1 | loop fusion | flops 9437184 | bytes 4265984 | tf_op jit(solution)/shard_map/while/body/eval_jaxpr/mul | solution.py:101
  107.2 1.4 %multiply_reduce_fusion.11 = f32[4,3,128]{2,1,0:T(4,128)S(1)} fusion(f32[4,8,128,128]{3,2,1,0:T(8,128)S(1)} %fusion.24, f32[4,8,3]{2,1,0:T(8,128)S(1)} %broadcast_multiply_fusion.5, f32[4,8,3,128]{3,2,1,0:T(4,128)S(1)} %slice.124, f32[4,3,128]{2,1,0:T(4,128)S(1)} %slice.125), kind=kLoop, calls=%fused_computation.17.clone.1 | loop fusion | flops 6289920 | bytes 2158976 | tf_op jit(solution)/shard_map/while/body/eval_jaxpr/reduce_sum | solution.py:105
  111.6 1.9 %fusion.24 = f32[4,8,128,128]{3,2,1,0:T(8,128)S(1)} fusion(f32[4,8,128,128]{3,2,1,0:T(8,128)S(1)} %multiply_reduce_fusion.10, f32[4,8,128]{2,1,0:T(8,128)S(1)} %bitcast.67, f32[4,8,128]{2,1,0:T(8,128)S(1)} %get-tuple-element.875, f32[4,8,128]{2,1,0:T(8,128)S(1)} %bitcast.68, f32[4,128]{1,0:T(4,128)S(1)} %bitcast.72, ...), kind=kLoop, calls=%fused_computation.25.clone.1 | loop fusion | flops 9437184 | bytes 4265984 | tf_op jit(solution)/shard_map/while/body/eval_jaxpr/mul | solution.py:101
  118.0 1.9 %fusion.24 = f32[4,8,128,128]{3,2,1,0:T(8,128)S(1)} fusion(f32[4,8,128,128]{3,2,1,0:T(8,128)S(1)} %multiply_reduce_fusion.10, f32[4,8,128]{2,1,0:T(8,128)S(1)} %bitcast.67, f32[4,8,128]{2,1,0:T(8,128)S(1)} %get-tuple-element.875, f32[4,8,128]{2,1,0:T(8,128)S(1)} %bitcast.68, f32[4,128]{1,0:T(4,128)S(1)} %bitcast.72, ...), kind=kLoop, calls=%fused_computation.25.clone.1 | loop fusion | flops 9437184 | bytes 4265984 | tf_op jit(solution)/shard_map/while/body/eval_jaxpr/mul | solution.py:101
  119.8 1.4 %multiply_reduce_fusion.11 = f32[4,3,128]{2,1,0:T(4,128)S(1)} fusion(f32[4,8,128,128]{3,2,1,0:T(8,128)S(1)} %fusion.24, f32[4,8,3]{2,1,0:T(8,128)S(1)} %broadcast_multiply_fusion.5, f32[4,8,3,128]{3,2,1,0:T(4,128)S(1)} %slice.124, f32[4,3,128]{2,1,0:T(4,128)S(1)} %slice.125), kind=kLoop, calls=%fused_computation.17.clone.1 | loop fusion | flops 6289920 | bytes 2158976 | tf_op jit(solution)/shard_map/while/body/eval_jaxpr/reduce_sum | solution.py:105
  124.3 1.9 %fusion.24 = f32[4,8,128,128]{3,2,1,0:T(8,128)S(1)} fusion(f32[4,8,128,128]{3,2,1,0:T(8,128)S(1)} %multiply_reduce_fusion.10, f32[4,8,128]{2,1,0:T(8,128)S(1)} %bitcast.67, f32[4,8,128]{2,1,0:T(8,128)S(1)} %get-tuple-element.875, f32[4,8,128]{2,1,0:T(8,128)S(1)} %bitcast.68, f32[4,128]{1,0:T(4,128)S(1)} %bitcast.72, ...), kind=kLoop, calls=%fused_computation.25.clone.1 | loop fusion | flops 9437184 | bytes 4265984 | tf_op jit(solution)/shard_map/while/body/eval_jaxpr/mul | solution.py:101
  (284 shorter events, 55.7 us)
Async XLA Ops:
  0.6 26.2 %copy-start.1 = (f32[3]{0:T(128)S(1)}, f32[3]{0:T(128)}, u32[]{:S(2)}) copy-start(f32[3]{0:T(128)} %constant.246.clone..sunk.6) | copy-start | bytes 40
  0.6 26.2 %copy-start.2 = (s32[4]{0:T(128)S(1)}, s32[4]{0:T(128)}, u32[]{:S(2)}) copy-start(s32[4]{0:T(128)} %param.12) | copy-start | bytes 52
  0.7 5.6 %collective-permute-start.1 = (f32[4,5,128]{2,0,1:T(4,128)}, f32[4,5,128]{2,0,1:T(4,128)S(1)}, u32[]{:S(2)}, u32[]{:S(2)}) collective-permute-start(f32[4,5,128]{2,0,1:T(4,128)} %param.9), channel_id=1, source_target_pairs={{8,0},{16,8},{24,16},{0,24},{9,1},{17,9},{25,17},{1,25},{10,2},{18... | collective-permute-start | bytes 30728 | tf_op jit(solution)/shard_map/ppermute | solution.py:38
  4.6 4.8 %collective-permute-start = (f32[4,5,128]{2,0,1:T(4,128)}, f32[4,5,128]{2,0,1:T(4,128)S(1)}, u32[]{:S(2)}, u32[]{:S(2)}) collective-permute-start(f32[4,5,128]{2,0,1:T(4,128)} %param.9), channel_id=1, source_target_pairs={{0,8},{8,16},{16,24},{24,0},{1,9},{9,17},{17,25},{25,1},{2,10},{10... | collective-permute-start | bytes 30728 | tf_op jit(solution)/shard_map/ppermute | solution.py:35
  10.1 1.3 %collective-permute-start.2 = (f32[1,12,5,128]{3,1,2,0:T(8,128)S(1)}, f32[1,12,5,128]{3,1,2,0:T(8,128)S(1)}, u32[]{:S(2)}, u32[]{:S(2)}) collective-permute-start(f32[1,12,5,128]{3,1,2,0:T(8,128)S(1)} %maximum_bitcast_fusion), channel_id=1, source_target_pairs={{0,1},{1,0},{2,3},{3,2},{4,5},{5,4},{6,7},{7,6},{8,9},{9,8},{10,11... | collective-permute-start | bytes 92168 | tf_op jit(solution)/shard_map/ppermute | solution.py:22
  12.2 4.6 %collective-permute-start.3 = (f32[2,12,5,128]{3,1,2,0:T(8,128)S(1)}, f32[2,12,5,128]{3,1,2,0:T(8,128)S(1)}, u32[]{:S(2)}, u32[]{:S(2)}) collective-permute-start(f32[2,12,5,128]{3,1,2,0:T(8,128)S(1)} %pad_maximum_fusion.2), channel_id=1, source_target_pairs={{0,2},{1,3},{2,0},{3,1},{4,6},{5,7},{6,4},{7,5},{8,10},{9,11},{10,... | collective-permute-start | bytes 184328 | tf_op jit(solution)/shard_map/ppermute | solution.py:22
  16.8 9.9 %collective-permute-start.4 = (f32[4,12,5,128]{3,1,2,0:T(8,128)S(1)}, f32[4,12,5,128]{3,1,2,0:T(8,128)S(1)}, u32[]{:S(2)}, u32[]{:S(2)}) collective-permute-start(f32[4,12,5,128]{3,1,2,0:T(8,128)S(1)} %pad_maximum_fusion.1), channel_id=1, source_target_pairs={{0,4},{1,5},{2,6},{3,7},{4,0},{5,1},{6,2},{7,3},{8,12},{9,13},{10,... | collective-permute-start | bytes 368648 | tf_op jit(solution)/shard_map/ppermute | solution.py:22
  26.8 31.4 %copy-start.3 = (f32[4,128]{1,0:T(4,128)S(1)}, f32[4,128]{1,0:T(4,128)}, u32[]{:S(2)}) copy-start(f32[4,128]{1,0:T(4,128)} %param.10) | copy-start | bytes 6148
  58.3 18.6 %copy-start = (f32[4,128]{1,0:T(4,128)}, f32[4,128]{1,0:T(4,128)S(1)}, u32[]{:S(2)}) copy-start(f32[4,128]{1,0:T(4,128)S(1)} %get-tuple-element.691) | copy-start | bytes 6148
  58.3 3.6 %collective-permute-start.6 = (f32[4,128]{1,0:T(4,128)S(1)}, f32[4,128]{1,0:T(4,128)S(1)}, u32[]{:S(2)}, u32[]{:S(2)}) collective-permute-start(f32[4,128]{1,0:T(4,128)S(1)} %multiply_divide_fusion), channel_id=1, source_target_pairs={{8,0},{16,8},{24,16},{0,24},{9,1},{17,9},{25,17},{1,25},{10,2},{18... | collective-permute-start | bytes 6152 | tf_op jit(solution)/shard_map/ppermute | solution.py:38
  58.4 4.5 %collective-permute-start.5 = (f32[4,128]{1,0:T(4,128)S(1)}, f32[4,128]{1,0:T(4,128)S(1)}, u32[]{:S(2)}, u32[]{:S(2)}) collective-permute-start(f32[4,128]{1,0:T(4,128)S(1)} %multiply_divide_fusion), channel_id=1, source_target_pairs={{0,8},{8,16},{16,24},{24,0},{1,9},{9,17},{17,25},{25,1},{2,10},{10... | collective-permute-start | bytes 6152 | tf_op jit(solution)/shard_map/ppermute | solution.py:35
